TPU v7x, 256 devices: a whole 4x4x8 slice. The times are simulated.
256 devices in a mesh: tile: 64 (over z, x, core), rot: 4 (over y).
Axes of the slice: x: 4, y: 4, z: 8, core: 2. Of those that a mesh axis runs over, the one named last changes fastest.
Arguments:
- tomogram: bfloat16 [2048, 5120], P('tile'), may hold values from -12 to 12
- templates: bfloat16 [16, 110592], P('rot', 'tile'), may hold values from -6 to 6
- valid: int32 [2048, 80], P('tile'), may hold values from 0 to 1, as said below
- quats: float32 [4, 4096], replicated, may hold values from -1 to 1, as said below
- rot_index: int32 [16], P('rot'), may hold values from 0 to 4095
Outputs:
- best: float32 [2048, 5120], P('tile', 'rot')
- evidence: float32 [2048, 5120], P('tile', 'rot')
- moments: float32 [4, 2048, 5120], P(None, 'tile', 'rot')
Inputs may be any that keep to these rules, and one draw needn't show every extreme that they name: `valid`: 1 marks a column (x, y) of voxels inside the lamella. `quats`: each column is a unit quaternion with a non-negative first component.
All inputs are finite; a program needn't handle non-finite values.
Results may differ from a plain program's by a relative error of at most 0.0003.
Values may be sent and summed in bfloat16 or wider, within the bound.
A program may use at most 128 MiB of HBM per device.

v0:
```python
import math
import jax
import jax.numpy as jnp
from jax import lax
from jax.sharding import PartitionSpec as P

TEMPL = 48
HALF = 24
EPSILON = 1e-06
TWO_PI = 2.0 * math.pi


def padded(block, sides, width):
    for axis, dim in sides:
        count = lax.axis_size(axis)
        forward = [(i, i + 1) for i in range(count - 1)]
        backward = [(target, source) for source, target in forward]
        low = lax.ppermute(
            lax.slice_in_dim(block, block.shape[dim] - width, None, axis=dim), axis, forward
        )
        high = lax.ppermute(lax.slice_in_dim(block, 0, width, axis=dim), axis, backward)
        block = jnp.concatenate([low, block, high], axis=dim)
    return block


def twiddle(count_in, shift_in, count_out, shift_out, length, direction, factor):
    row_idx = (jnp.arange(count_in, dtype=jnp.int32) + shift_in)[:, None]
    col_idx = (jnp.arange(count_out, dtype=jnp.int32) + shift_out)[None, :]
    phase_idx = jnp.remainder(row_idx * col_idx, length).astype(jnp.float32)
    angles = phase_idx * jnp.float32(direction * TWO_PI / length)
    real_part = jnp.cos(angles) * factor
    imag_part = jnp.sin(angles) * factor
    upper_half = jnp.stack([real_part, imag_part], axis=1)
    lower_half = jnp.stack([-imag_part, real_part], axis=1)
    return jnp.stack([upper_half, lower_half], axis=0)


def product(formula, left_arr, right_arr):
    return jnp.einsum(
        formula,
        left_arr,
        right_arr,
        precision=lax.Precision.HIGH,
        preferred_element_type=jnp.float32,
    )


def forward(volume, shift, direction, lengths):
    size_x, size_y, size_z = volume.shape
    table_z = twiddle(size_z, shift, lengths[2], 0, lengths[2], direction, 1.0)[0]
    spectrum = product("xyz,zdk->dxyk", volume, table_z)
    spectrum = product(
        "cxyz,cydk->dxkz",
        spectrum,
        twiddle(size_y, shift, lengths[1], 0, lengths[1], direction, 1.0),
    )
    return product(
        "cxyz,cxdk->dkyz",
        spectrum,
        twiddle(size_x, shift, lengths[0], 0, lengths[0], direction, 1.0),
    )


def inverse(spectrum, out_x, out_y, out_z, lengths):
    spectrum = product(
        "cxyz,cxdk->dkyz",
        spectrum,
        twiddle(lengths[0], 0, out_x, HALF, lengths[0], 1, 1.0 / lengths[0]),
    )
    spectrum = product(
        "cxyz,cydk->dxkz",
        spectrum,
        twiddle(lengths[1], 0, out_y, 0, lengths[1], 1, 1.0 / lengths[1]),
    )
    real_table = twiddle(lengths[2], 0, out_z, 0, lengths[2], 1, 1.0 / lengths[2])[:, :, 0]
    return product("cxyz,czk->xyk", spectrum, real_table)


def multiply(first_arr, other_arr):
    return jnp.stack(
        [
            first_arr[0] * other_arr[0] - first_arr[1] * other_arr[1],
            first_arr[0] * other_arr[1] + first_arr[1] * other_arr[0],
        ]
    )


def local(tomogram, templates, valid, quats, rot_index):
    x_cells, voxels = tomogram.shape
    y_cells = valid.shape[1]
    z_cells = voxels // y_cells
    lengths = (x_cells + TEMPL, y_cells + HALF, z_cells + HALF)
    widened = padded(tomogram, (("tile", 0),), HALF)
    slab_spectrum = forward(
        widened.astype(jnp.float32).reshape(x_cells + TEMPL, y_cells, z_cells), 0, -1, lengths
    )
    gathered_bank = lax.all_gather(templates, "tile", axis=1, tiled=True).astype(jnp.float32)
    centred = gathered_bank - jnp.mean(gathered_bank, axis=1, keepdims=True)
    tmpl_spread = jnp.sqrt(jnp.mean(centred * centred, axis=1, keepdims=True) + EPSILON)
    unit_bank = centred / (tmpl_spread * jnp.float32(TEMPL) ** 1.5)

    def correlate(unit_tmpl):
        tmpl_spectrum = forward(unit_tmpl.reshape(TEMPL, TEMPL, TEMPL), -HALF, 1, lengths)
        return inverse(multiply(slab_spectrum, tmpl_spectrum), x_cells, y_cells, z_cells, lengths)

    correlation = lax.map(correlate, unit_bank).reshape(unit_bank.shape[0], x_cells, voxels)
    inside = jnp.repeat(valid.astype(jnp.float32), z_cells, axis=1)
    columns = jnp.sum(valid.astype(jnp.float32))
    masked = correlation * inside[None]
    first_sum, all_columns = lax.psum((jnp.sum(masked, axis=(1, 2)), columns), "tile")
    voxel_count = all_columns * z_cells
    average = first_sum / voxel_count
    deviation = correlation - average[:, None, None]
    square_sum = lax.psum(jnp.sum(inside[None] * deviation * deviation, axis=(1, 2)), "tile")
    spread = jnp.sqrt(square_sum / voxel_count + EPSILON)
    scores = (correlation - average[:, None, None]) / spread[:, None, None]
    one_hot = (rot_index[:, None] == jnp.arange(quats.shape[1], dtype=jnp.int32)[None, :]).astype(
        jnp.float32
    )
    orient = product("rq,kq->rk", one_hot, quats)
    highest = jnp.max(scores, axis=0)
    weight = jnp.exp(scores - highest[None])
    exp_total = jnp.sum(weight, axis=0)
    moment = product("rxv,rk->kxv", weight, orient)
    groups = lax.axis_size("rot")
    share_len = voxels // groups
    offset = lax.axis_index("rot") * share_len
    high_full = lax.pmax(highest, "rot")
    rescale = jnp.exp(highest - high_full)
    total_full, moment_full = lax.psum((exp_total * rescale, moment * rescale[None]), "rot")
    high_all = lax.dynamic_slice_in_dim(high_full, offset, share_len, 1)
    total_all = lax.dynamic_slice_in_dim(total_full, offset, share_len, 1)
    moment_all = lax.dynamic_slice_in_dim(moment_full, offset, share_len, 2)
    inside_part = lax.dynamic_slice_in_dim(inside, offset, share_len, 1)
    best = inside_part * high_all
    evidence = inside_part * (high_all + jnp.log(total_all))
    moments = inside_part[None] * moment_all / total_all[None]
    return (best, evidence, moments)


def solution(mesh):
    placed = (P("tile", None), P("rot", "tile"), P("tile", None), P(), P("rot"))
    return jax.shard_map(
        local,
        mesh=mesh,
        in_specs=placed,
        out_specs=(P("tile", "rot"), P("tile", "rot"), P(None, "tile", "rot")),
        check_vma=False,
    )
```

profile of v0, /device:TPU:1, one launch (start us, length us, event | category | flops | bytes accessed | tf_op | source)
XLA Modules:
  0.0 683.0 jit_solution(3317119279552520776)
XLA Ops:
  16.4 55.7 %all-gather = bf16[64,1728,4]{1,2,0:T(4,128)(2,1)S(1)} all-gather(bf16[1,1728,4]{1,2,0:T(4,128)(2,1)} %bitcast.196), channel_id=1, replica_groups=mesh['tile'=64,'rot'=4] {'tile'}, dimensions={0}, use_global_device_ids=true | all-gather | bytes 898560 | tf_op jit(solution)/shard_map/all_gather | solution.py:97
  84.1 4.6 convolution_bitcast_fusion.1
  88.8 9.4 %copy.71 = f32[2,80,80,88,1]{2,1,0,4,3:T(8,128)} copy(f32[2,80,80,88,1]{3,2,1,0,4:T(8,128)} %convolution_bitcast_fusion.1) | data formatting | bytes 9011200 | tf_op jit(solution)/shard_map/xyz,zdk->dxyk/transpose | solution.py:39
  98.2 5.5 fusion.90
  103.7 5.6 fusion.83
  109.3 145.3 %while.13 = (s32[]{:T(128)}, f32[4,32,80,64]{2,3,1,0:T(8,128)}, f32[2,80,104,88]{2,1,3,0:T(8,128)}, f32[4,110592]{1,0:T(4,128)}, s32[]{:T(128)}) while((s32[]{:T(128)}, f32[4,32,80,64]{2,3,1,0:T(8,128)}, f32[2,80,104,88]{2,1,3,0:T(8,128)}, f32[4,110592]{1,0:T(4,128)}, s32[]{:T(128)}) %tuple.86), condition=%wide.region_3.4_spmd, body=%wide.region_2.3_spmd.sunk | while | flops 2770436608 | bytes 55842368 | solution.py:106
  116.4 4.6 copy.104
  128.1 5.9 multiply_subtract_fusion.2
  134.2 4.5 fusion.161
  152.7 4.6 copy.104
  164.4 5.9 multiply_subtract_fusion.2
  170.5 4.5 fusion.161
  188.9 4.6 copy.104
  200.6 5.9 multiply_subtract_fusion.2
  206.7 4.5 fusion.161
  225.1 4.6 copy.104
  236.8 5.9 multiply_subtract_fusion.2
  257.7 124.2 %all-reduce = (f32[4]{0:T(128)S(1)}, f32[]{:T(128)}) all-reduce(f32[4]{0:T(128)S(1)} %multiply_reduce_fusion, f32[]{:T(128)} %convert_reduce_fusion.1), channel_id=1, replica_groups=mesh['tile'=64,'rot'=4] {'tile'}, use_global_device_ids=true, to_apply=%region_5.6 | all-reduce | flops 5 | bytes 40 | tf_op jit(solution)/shard_map/psum | solution.py:110
  385.7 5.7 copy.55
  391.4 126.6 %psum.37 = f32[4]{0:T(128)S(1)} all-reduce(f32[4]{0:T(128)S(1)} %fusion.82), channel_id=1, replica_groups=mesh['tile'=64,'rot'=4] {'tile'}, use_global_device_ids=true, to_apply=%region_9.10 | all-reduce | flops 4 | bytes 32 | tf_op jit(solution)/shard_map/psum | solution.py:114
  527.1 5.4 reshape.768
  536.5 41.4 %all-reduce.5.cloned.1.call-done = f32[32,5120]{1,0:T(8,128)} async-done(((f32[32,5120]{1,0:T(8,128)}), f32[32,5120]{1,0:T(8,128)}) %all-reduce.5.cloned.1.call-update) | async-done | bytes 655376 | tf_op jit(solution)/shard_map/pmax | solution.py:128
  580.1 5.6 convolution_multiply_fusion
  586.6 85.2 %all-reduce.7.cloned.1.call-done = (f32[32,5120]{1,0:T(8,128)}, f32[4,32,5120]{2,0,1:T(4,128)}) async-done(((f32[32,5120]{1,0:T(8,128)}, f32[4,32,5120]{2,0,1:T(4,128)}), (f32[32,5120]{1,0:T(8,128)}, f32[4,32,5120]{2,0,1:T(4,128)})) %all-reduce.7.cloned.1.call-update) | async-done | bytes 3276816 | tf_op jit(solution)/shard_map/psum | solution.py:130
  (149 shorter events, 136.4 us)
Async XLA Ops:
  7.2 250.3 %copy-start = (f32[4,4096]{1,0:T(4,128)S(1)}, f32[4,4096]{1,0:T(4,128)}, u32[]{:S(2)}) copy-start(f32[4,4096]{1,0:T(4,128)} %param.10) | copy-start | bytes 196612
  7.2 570.7 %all-reduce.5.cloned.1.call-start = ((), (), s32[]{:S(2)}) async-start(), calls=%async_computation | async-start | bytes 1310720 | tf_op jit(solution)/shard_map/pmax | solution.py:128
  9.0 71.8 %collective-permute-start = (bf16[24,5120]{1,0:T(8,128)(2,1)}, bf16[24,5120]{1,0:T(8,128)(2,1)S(1)}, u32[]{:S(2)}, u32[]{:S(2)}) collective-permute-start(bf16[24,5120]{1,0:T(8,128)(2,1)} %get-tuple-element.138), channel_id=1, source_target_pairs={{0,4},{4,8},{8,12},{12,16},{16,20},{20,24},{24,28},{28,32},{32,36}... | collective-permute-start | bytes 737288 | tf_op jit(solution)/shard_map/ppermute | solution.py:18
  13.5 68.0 %collective-permute-start.1 = (bf16[24,5120]{1,0:T(8,128)(2,1)S(1)}, bf16[24,5120]{1,0:T(8,128)(2,1)}, u32[]{:S(2)}, u32[]{:S(2)}) collective-permute-start(bf16[24,5120]{1,0:T(8,128)(2,1)S(1)} %get-tuple-element.139), channel_id=1, source_target_pairs={{4,0},{8,4},{12,8},{16,12},{20,16},{24,20},{28,24},{32,28},{36,32}... | collective-permute-start | bytes 737288 | tf_op jit(solution)/shard_map/ppermute | solution.py:21
  74.6 5.6 copy-start.5
  77.4 4.1 copy-start.3
  80.8 0.7 copy-start.4
  254.6 2.9 copy-start.6
  527.1 5.4 copy-start.2
  532.5 1.7 copy-start.1
  534.2 137.5 %all-reduce.7.cloned.1.call-start = ((), (), s32[]{:S(2)}) async-start(), calls=%async_computation.1 | async-start | bytes 6553600 | tf_op jit(solution)/shard_map/psum | solution.py:130
Sparse Core Ops, SparseCore 0:
  534.3 43.5 all-reduce.4
  585.9 85.7 all-reduce.6
where the time goes:
time: 690 us; the launch traced here: 683 us
  blocking collectives  307 us (44%)
  waiting for transfers between devices  127 us (18%)
  matrix products  101 us (15%)
  local copies, waits for them, and re-layouts  69.1 us (10%)
  other arithmetic  56.8 us (8%)
  between operations  15.3 us (2%)
    psum x1, blocking collectives, local(): lax.psum(jnp.sum(inside[None] * deviation * deviation, axis=(1, 2)), 'tile')  127 us
    psum x1, blocking collectives, local(): lax.psum((jnp.sum(masked, axis=(1, 2)), columns), 'tile')  124 us
    dot_general x29, matrix products, product(): jnp.einsum(formula, left_arr, right_arr, precision=lax.Precision.HIGH, pr...  101 us
    psum x1, waiting for transfers between devices, local(): lax.psum((exp_total * rescale, moment * rescale[None]), 'rot')  85.2 us
    all_gather x1, blocking collectives, local(): lax.all_gather(templates, 'tile', axis=1, tiled=True).astype(jnp.float32)  55.7 us
    pmax x1, waiting for transfers between devices, local(): high_full = lax.pmax(highest, 'rot')  41.4 us
    transpose x5, local copies, waits for them, and re-layouts, product(): jnp.einsum(formula, left_arr, right_arr, precision=lax.Precision.HIGH, pr...  27.7 us
    sub x4, other arithmetic, multiply(): first_arr[0] * other_arr[0] - first_arr[1] * other_arr[1]  23.7 us
  transfers between devices with their start and end apart: 4, of which 2 were waited for; matrix products, arithmetic and copies ran while one was open for 2% of the time, Pallas kernels for 0%

commit v1 on v0

--- a/solution.py
+++ b/solution.py
@@ -8,6 +8,12 @@
 HALF = 24
 EPSILON = 1e-06
 TWO_PI = 2.0 * math.pi
+
+
+def gather_from_all(x, axis, dim):
+    count = lax.axis_size(axis)
+    repeats = [count if d == dim else 1 for d in range(x.ndim)]
+    return lax.all_to_all(jnp.tile(x, repeats), axis, split_axis=dim, concat_axis=dim, tiled=True)
 
 
 def padded(block, sides, width):
@@ -94,7 +100,7 @@
     slab_spectrum = forward(
         widened.astype(jnp.float32).reshape(x_cells + TEMPL, y_cells, z_cells), 0, -1, lengths
     )
-    gathered_bank = lax.all_gather(templates, "tile", axis=1, tiled=True).astype(jnp.float32)
+    gathered_bank = gather_from_all(templates, "tile", 1).astype(jnp.float32)
     centred = gathered_bank - jnp.mean(gathered_bank, axis=1, keepdims=True)
     tmpl_spread = jnp.sqrt(jnp.mean(centred * centred, axis=1, keepdims=True) + EPSILON)
     unit_bank = centred / (tmpl_spread * jnp.float32(TEMPL) ** 1.5)

time: 690 us -> 659 us (0.955)
  blocking collectives: 307 us -> 253 us
  starting transfers between devices: 6.52 us -> 19.5 us
  loops' own time: 0.79 us -> 12.2 us
  local copies, waits for them, and re-layouts: 69.1 us -> 61.9 us
    all_gather x1 -> x0, blocking collectives: 55.7 us -> none  [local(): lax.all_gather(templates, 'tile', axis=1, tiled=True).astype(jnp.float32)]
    all_to_all x0 -> x1, starting transfers between devices: none -> 13 us  [gather_from_all(): lax.all_to_all(jnp.tile(x, repeats), axis, split_axis=dim, concat_axis=di...]
    another operation x1, loops' own time: 0.79 us -> 12.2 us  [local(): lax.map(correlate, unit_bank).reshape(unit_bank.shape[0], x_cells, voxels)]
  transfers between devices with their start and end apart: 4 -> 5, of which waited for: 2 -> 2; matrix products, arithmetic and copies ran while one was open for 2% -> 5% of each run, Pallas kernels for 0% -> 0%
where the time goes in v1:
time: 659 us; the launch traced here: 649 us
  blocking collectives  253 us (38%)
  waiting for transfers between devices  126 us (19%)
  matrix products  102 us (15%)
  local copies, waits for them, and re-layouts  61.9 us (9%)
  other arithmetic  58 us (9%)
  starting transfers between devices  19.5 us (3%)
  between operations  15.3 us (2%)
  loops' own time  12.2 us (2%)
    psum x1, blocking collectives, local(): lax.psum(jnp.sum(inside[None] * deviation * deviation, axis=(1, 2)), 'tile')  129 us
    psum x1, blocking collectives, local(): lax.psum((jnp.sum(masked, axis=(1, 2)), columns), 'tile')  125 us
    dot_general x29, matrix products, product(): jnp.einsum(formula, left_arr, right_arr, precision=lax.Precision.HIGH, pr...  102 us
    psum x1, waiting for transfers between devices, local(): lax.psum((exp_total * rescale, moment * rescale[None]), 'rot')  85.2 us
    pmax x1, waiting for transfers between devices, local(): high_full = lax.pmax(highest, 'rot')  41.1 us
    transpose x5, local copies, waits for them, and re-layouts, product(): jnp.einsum(formula, left_arr, right_arr, precision=lax.Precision.HIGH, pr...  27.7 us
    sub x4, other arithmetic, multiply(): first_arr[0] * other_arr[0] - first_arr[1] * other_arr[1]  23.6 us
  transfers between devices with their start and end apart: 5, of which 2 were waited for; matrix products, arithmetic and copies ran while one was open for 5% of the time, Pallas kernels for 0%

profile of v1, /device:TPU:1, one launch (start us, length us, event | category | flops | bytes accessed | tf_op | source)
XLA Modules:
  0.0 648.7 jit_solution(13567034579072992435)
XLA Ops:
  8.4 4.5 collective-permute-start
  16.7 13.0 %all-to-all-start = ((bf16[4,64,1728]{2,0,1:T(4,128)(2,1)}), bf16[4,64,1728]{2,0,1:T(4,128)(2,1)S(1)}, u32[]{:S(2)}, u32[]{:S(2)}) async-start(bf16[4,64,1728]{2,0,1:T(4,128)(2,1)} %tile.2), calls=%async_computation | async-start | bytes 1835008 | tf_op jit(solution)/shard_map/all_to_all | solution.py:16
  34.4 5.4 convolution_bitcast_fusion.1
  39.8 9.4 %copy.69 = f32[2,80,80,88,1]{2,1,0,4,3:T(8,128)} copy(f32[2,80,80,88,1]{3,2,1,0,4:T(8,128)} %convolution_bitcast_fusion.1) | data formatting | bytes 9011200 | tf_op jit(solution)/shard_map/xyz,zdk->dxyk/transpose | solution.py:45
  49.2 5.5 fusion.90
  54.8 5.6 fusion.83
  67.3 150.8 %while.13 = (s32[]{:T(128)}, f32[4,32,80,64]{2,3,1,0:T(8,128)}, f32[2,80,104,88]{2,1,3,0:T(8,128)}, f32[4,110592]{1,0:T(4,128)S(1)}, s32[]{:T(128)}) while((s32[]{:T(128)}, f32[4,32,80,64]{2,3,1,0:T(8,128)}, f32[2,80,104,88]{2,1,3,0:T(8,128)}, f32[4,110592]{1,0:T(4,128)S(1)}, s32[]{:T(128)}) %tuple.86), condition=%wide.region_3.4_spmd, body=%wide.region_2.3_spmd.sunk | while | flops 2770436608 | bytes 69998200 | solution.py:112
  84.4 4.6 copy.102
  96.1 5.9 multiply_subtract_fusion.2
  102.2 4.5 fusion.161
  119.2 4.6 copy.102
  130.9 5.9 multiply_subtract_fusion.2
  154.0 4.6 copy.102
  165.7 5.9 multiply_subtract_fusion.2
  171.8 4.5 fusion.161
  188.8 4.6 copy.102
  200.5 5.9 multiply_subtract_fusion.2
  221.2 124.6 %all-reduce = (f32[4]{0:T(128)S(1)}, f32[]{:T(128)}) all-reduce(f32[4]{0:T(128)S(1)} %multiply_reduce_fusion, f32[]{:T(128)} %convert_reduce_fusion.1), channel_id=1, replica_groups=mesh['tile'=64,'rot'=4] {'tile'}, use_global_device_ids=true, to_apply=%region_5.6 | all-reduce | flops 5 | bytes 40 | tf_op jit(solution)/shard_map/psum | solution.py:116
  349.6 5.7 copy.53
  355.2 128.7 %psum.37 = f32[4]{0:T(128)S(1)} all-reduce(f32[4]{0:T(128)S(1)} %fusion.82), channel_id=1, replica_groups=mesh['tile'=64,'rot'=4] {'tile'}, use_global_device_ids=true, to_apply=%region_9.10 | all-reduce | flops 4 | bytes 32 | tf_op jit(solution)/shard_map/psum | solution.py:120
  493.0 5.4 reshape.782
  502.4 41.1 %all-reduce.5.cloned.1.call-done = f32[32,5120]{1,0:T(8,128)} async-done(((f32[32,5120]{1,0:T(8,128)}), f32[32,5120]{1,0:T(8,128)}) %all-reduce.5.cloned.1.call-update) | async-done | bytes 655376 | tf_op jit(solution)/shard_map/pmax | solution.py:134
  545.8 5.6 convolution_multiply_fusion
  552.2 85.2 %all-reduce.7.cloned.1.call-done = (f32[32,5120]{1,0:T(8,128)}, f32[4,32,5120]{2,0,1:T(4,128)}) async-done(((f32[32,5120]{1,0:T(8,128)}, f32[4,32,5120]{2,0,1:T(4,128)}), (f32[32,5120]{1,0:T(8,128)}, f32[4,32,5120]{2,0,1:T(4,128)})) %all-reduce.7.cloned.1.call-update) | async-done | bytes 3276816 | tf_op jit(solution)/shard_map/psum | solution.py:136
  (171 shorter events, 130.4 us)
Async XLA Ops:
  7.2 213.7 %copy-start = (f32[4,4096]{1,0:T(4,128)S(1)}, f32[4,4096]{1,0:T(4,128)}, u32[]{:S(2)}) copy-start(f32[4,4096]{1,0:T(4,128)} %param.10) | copy-start | bytes 196612
  7.2 26.1 %copy-start.5 = (bf16[32,5120]{1,0:T(8,128)(2,1)S(1)}, bf16[32,5120]{1,0:T(8,128)(2,1)}, u32[]{:S(2)}) copy-start(bf16[32,5120]{1,0:T(8,128)(2,1)} %param.7) | copy-start | bytes 983044
  7.2 24.1 %copy-start.9 = (s32[32,80]{1,0:T(8,128)S(1)}, s32[32,80]{1,0:T(8,128)}, u32[]{:S(2)}) copy-start(s32[32,80]{1,0:T(8,128)} %param.9) | copy-start | bytes 30724
  8.4 24.9 %collective-permute-start = (bf16[24,5120]{1,0:T(8,128)(2,1)S(1)}, bf16[24,5120]{1,0:T(8,128)(2,1)S(1)}, u32[]{:S(2)}, u32[]{:S(2)}) collective-permute-start(bf16[24,5120]{1,0:T(8,128)(2,1)S(1)} %get-tuple-element.138), channel_id=1, source_target_pairs={{0,4},{4,8},{8,12},{12,16},{16,20},{20,24},{24,28},{28,32},{32,36}... | collective-permute-start | bytes 737288 | tf_op jit(solution)/shard_map/ppermute | solution.py:24
  12.9 20.4 %collective-permute-start.1 = (bf16[24,5120]{1,0:T(8,128)(2,1)S(1)}, bf16[24,5120]{1,0:T(8,128)(2,1)S(1)}, u32[]{:S(2)}, u32[]{:S(2)}) collective-permute-start(bf16[24,5120]{1,0:T(8,128)(2,1)S(1)} %get-tuple-element.139), channel_id=1, source_target_pairs={{4,0},{8,4},{12,8},{16,12},{20,16},{24,20},{28,24},{32,28},{36,32}... | collective-permute-start | bytes 737288 | tf_op jit(solution)/shard_map/ppermute | solution.py:27
  16.7 43.7 %all-to-all-start = ((bf16[4,64,1728]{2,0,1:T(4,128)(2,1)}), bf16[4,64,1728]{2,0,1:T(4,128)(2,1)S(1)}, u32[]{:S(2)}, u32[]{:S(2)}) async-start(bf16[4,64,1728]{2,0,1:T(4,128)(2,1)} %tile.2), calls=%async_computation | async-start | bytes 1835008 | tf_op jit(solution)/shard_map/all_to_all | solution.py:16
  29.7 513.8 %all-reduce.5.cloned.1.call-start = ((), (), s32[]{:S(2)}) async-start(), calls=%async_computation.1 | async-start | bytes 1310720 | tf_op jit(solution)/shard_map/pmax | solution.py:134
  39.8 9.4 %copy-start.6 = (f32[1,80,2,104]{3,1,0,2:T(8,128)S(1)}, f32[1,80,2,104]{3,1,0,2:T(8,128)}, u32[]{:S(2)}) copy-start(f32[1,80,2,104]{3,1,0,2:T(8,128)} %get-tuple-element.143) | copy-start | bytes 199684
  49.2 5.6 copy-start.7
  49.2 5.6 copy-start.8
  78.9 3.2 copy-start.2
  107.1 6.5 %copy-start.3 = (f32[4,110592]{1,0:T(4,128)S(1)}, f32[4,110592]{1,0:T(4,128)}, u32[]{:S(2)}) copy-start(f32[4,110592]{1,0:T(4,128)} %copy-done.2) | copy-start | bytes 5308420 | tf_op jit(solution)/shard_map/while
  113.7 3.2 copy-start.2
  141.9 6.6 %copy-start.3 = (f32[4,110592]{1,0:T(4,128)S(1)}, f32[4,110592]{1,0:T(4,128)}, u32[]{:S(2)}) copy-start(f32[4,110592]{1,0:T(4,128)} %copy-done.2) | copy-start | bytes 5308420 | tf_op jit(solution)/shard_map/while
  148.5 3.2 copy-start.2
  176.7 6.6 %copy-start.3 = (f32[4,110592]{1,0:T(4,128)S(1)}, f32[4,110592]{1,0:T(4,128)}, u32[]{:S(2)}) copy-start(f32[4,110592]{1,0:T(4,128)} %copy-done.2) | copy-start | bytes 5308420 | tf_op jit(solution)/shard_map/while
  183.3 3.2 copy-start.2
  211.5 6.6 %copy-start.3 = (f32[4,110592]{1,0:T(4,128)S(1)}, f32[4,110592]{1,0:T(4,128)}, u32[]{:S(2)}) copy-start(f32[4,110592]{1,0:T(4,128)} %copy-done.2) | copy-start | bytes 5308420 | tf_op jit(solution)/shard_map/while
  218.1 2.9 copy-start.10
  493.0 5.4 copy-start.4
  498.4 1.7 copy-start.1
  500.1 137.3 %all-reduce.7.cloned.1.call-start = ((), (), s32[]{:S(2)}) async-start(), calls=%async_computation.2 | async-start | bytes 6553600 | tf_op jit(solution)/shard_map/psum | solution.py:136
Sparse Core Ops, SparseCore 0:
  500.2 43.2 all-reduce.4
  551.6 85.7 all-reduce.6
